TPU v7x, 32 devices: a whole 2x2x4 slice. The times are simulated.
32 devices in a mesh: group: 2 (over x), area: 16 (over z, y, core).
Axes of the slice: x: 2, y: 2, z: 4, core: 2. Of those that a mesh axis runs over, the one named last changes fastest.
Arguments:
- state_init: float32 [64, 12288], P('group', 'area'), parts along dimension 0, may hold values from -6 to 6
- prior_interval_trace: bfloat16 [4, 64, 12288], P(None, 'group', 'area'), parts along dimension 1, may hold values from -0.8984375 to 0.8984375
- drive_input: bfloat16 [64, 12288], P('group', 'area'), parts along dimension 0, may hold values from -4 to 4
- leak_rate: float32 [24576], P(('group', 'area')), parts along dimension 0, may hold values from 0.15 to 1
- w_recur: bfloat16 [24576, 6144], P(('group', 'area')), parts along dimension 0, may hold values from -0.078125 to 0.078125
- w_send: bfloat16 [24576, 768], P(('group', 'area')), parts along dimension 0, may hold values from -0.078125 to 0.078125
- w_recv: bfloat16 [24576, 768], P(('group', 'area')), parts along dimension 0, may hold values from -0.21875 to 0.21875
- area_mask: int32 [4, 2], P('group'), parts along dimension 0, may hold values 0 or 1
- coupling: float32 [4, 2], P('group'), parts along dimension 0, may hold values from 0.1 to 0.6
- delay_slot: int32 [4, 2], P('group'), parts along dimension 0, may hold values from 0 to 3
Outputs:
- final_state: float32 [64, 12288], P('group', 'area'), parts along dimension 0
- final_history: bfloat16 [4, 64, 12288], P(None, 'group', 'area'), parts along dimension 1
There are 2 independent parts, one for each index of `group`. A program takes and returns all parts, laid end to end along the dimension named above; each array names one. Nothing has to cross between parts.
All inputs are finite; a program needn't handle non-finite values.
Results may differ from a plain program's by a relative error of at most 0.0095.
Values may be sent and summed in bfloat16 or wider, within the bound.
No kernel may reach another device: no remote copies, remote signals or barrier semaphores. Data moves between devices by JAX's collectives and lax.ppermute only.
A program may use at most 64 MiB of HBM per device.

v0:
```python
import jax
import jax.numpy as jnp
from jax import lax
from jax.sharding import PartitionSpec as P

SPLIT = 8
INTERVALS = 2


def from_partner(block, axis, bit):
    count = lax.axis_size(axis)
    route = []
    for low in range(count):
        high = low | 1 << bit
        if high != low and high < count:
            route += [(low, high), (high, low)]
    return lax.ppermute(block, axis, route)


def gather_region_activity(spiking_activity):
    device_index = lax.axis_index("area")
    gathered_activity = spiking_activity
    for bit_number in range(SPLIT.bit_length() - 1):
        partner = from_partner(gathered_activity, "area", bit_number)
        upper_half = device_index // 2**bit_number % 2
        gathered_activity = jnp.where(
            upper_half == 1,
            jnp.concatenate([partner, gathered_activity], 1),
            jnp.concatenate([gathered_activity, partner], 1),
        )
    return gathered_activity


def reduce_history(contrib):
    device_index = lax.axis_index("area")
    levels = (lax.axis_size("area") // SPLIT).bit_length() - 1
    for level in reversed(range(levels)):
        half_count = contrib.shape[0] // 2
        upper_half = device_index // (SPLIT * 2**level) % 2
        keeping = jnp.where(upper_half == 1, contrib[half_count:], contrib[:half_count])
        sending = jnp.where(upper_half == 1, contrib[:half_count], contrib[half_count:])
        partner = from_partner(sending, "area", SPLIT.bit_length() - 1 + level)
        contrib = keeping + partner
    return contrib[0]


def body(
    state_init,
    prior_interval_trace,
    drive_input,
    leak_rate,
    w_recur,
    w_send,
    w_recv,
    area_mask,
    coupling,
    delay_slot,
):
    device_index = lax.axis_index("area")
    my_area = device_index // SPLIT
    overall_ticks = prior_interval_trace.shape[0]
    trials_count = prior_interval_trace.shape[1]
    strength = area_mask.astype(jnp.float32) * coupling
    slots = jnp.arange(overall_ticks, dtype=jnp.int32)
    drive = drive_input.astype(jnp.float32)
    part_bits = SPLIT.bit_length() - 1
    neuron_voltage = state_init
    history = prior_interval_trace
    spiking_activity = prior_interval_trace[overall_ticks - 1]
    for interval in range(INTERVALS):
        flat = history.reshape(overall_ticks * trials_count, history.shape[2])
        partial_value = jnp.dot(flat, w_send, preferred_element_type=jnp.float32).reshape(
            overall_ticks, trials_count, w_send.shape[1]
        )
        column = lax.dynamic_index_in_dim(strength, my_area, 1, keepdims=False)
        lagging = lax.dynamic_index_in_dim(delay_slot, my_area, 1, keepdims=False)
        selector = (lagging[:, None] == slots[None, :]).astype(jnp.float32) * column[:, None]
        contrib = jnp.einsum(
            "ak,ktr->atr", selector, partial_value, precision=lax.Precision.HIGHEST
        )
        summed = reduce_history(contrib)
        for bit_number in range(part_bits):
            summed = summed + from_partner(summed, "area", bit_number)
        remote = lax.dot_general(
            summed.astype(jnp.bfloat16),
            w_recv,
            (((1,), (1,)), ((), ())),
            preferred_element_type=jnp.float32,
        )
        logged_activity = []
        for step_index in range(overall_ticks):
            gathered_activity = gather_region_activity(spiking_activity)
            lateral_forcing = lax.dot_general(
                gathered_activity,
                w_recur,
                (((1,), (1,)), ((), ())),
                preferred_element_type=jnp.float32,
            )
            neuron_voltage = neuron_voltage + leak_rate[None, :] * (
                -neuron_voltage + lateral_forcing + remote + drive
            )
            spiking_activity = jnp.tanh(neuron_voltage).astype(jnp.bfloat16)
            logged_activity.append(spiking_activity)
        history = jnp.stack(logged_activity)
    return (neuron_voltage, history)


def solution(mesh):
    in_specs = (
        P("group", "area"),
        P(None, "group", "area"),
        P("group", "area"),
        P(("group", "area")),
        P(("group", "area"), None),
        P(("group", "area"), None),
        P(("group", "area"), None),
        P("group", None),
        P("group", None),
        P("group", None),
    )
    out_specs = (P("group", "area"), P(None, "group", "area"))
    return jax.shard_map(body, mesh=mesh, in_specs=in_specs, out_specs=out_specs, check_vma=False)
```

profile of v0, /device:TPU:0, one launch (start us, length us, event | category | flops | bytes accessed | tf_op | source)
XLA Modules:
  0.0 156.7 jit_solution(16835788837397637880)
XLA Ops:
  4.9 4.1 %collective-permute-start.3 = (f32[1,32,768]{2,0,1:T(1,128)S(1)}, f32[1,32,768]{2,0,1:T(1,128)S(1)}, u32[]{:S(2)}, u32[]{:S(2)}) collective-permute-start(f32[1,32,768]{2,0,1:T(1,128)S(1)} %broadcast_select_fusion.2), channel_id=1, source_target_pairs={{0,8},{8,0},{1,9},{9,1},{2,10},{10,2},{3,11},{11,3},{4,12},{12,4},... | collective-permute-start | bytes 294920 | tf_op jit(solution)/shard_map/ppermute | solution.py:17
  9.0 4.9 %collective-permute-done.3 = f32[1,32,768]{2,0,1:T(1,128)S(1)} collective-permute-done((f32[1,32,768]{2,0,1:T(1,128)S(1)}, f32[1,32,768]{2,0,1:T(1,128)S(1)}, u32[]{:S(2)}, u32[]{:S(2)}) %collective-permute-start.3) | collective-permute-done | bytes 98336 | tf_op jit(solution)/shard_map/ppermute | solution.py:17
  18.0 3.1 %collective-permute-done.5 = f32[32,768]{1,0:T(8,128)S(1)} collective-permute-done((f32[32,768]{1,0:T(8,128)S(1)}, f32[32,768]{1,0:T(8,128)S(1)}, u32[]{:S(2)}, u32[]{:S(2)}) %collective-permute-start.5) | collective-permute-done | bytes 98336 | tf_op jit(solution)/shard_map/ppermute | solution.py:17
  23.4 3.5 %collective-permute-done.6 = f32[32,768]{1,0:T(8,128)S(1)} collective-permute-done((f32[32,768]{1,0:T(8,128)S(1)}, f32[32,768]{1,0:T(8,128)S(1)}, u32[]{:S(2)}, u32[]{:S(2)}) %collective-permute-start.6) | collective-permute-done | bytes 98336 | tf_op jit(solution)/shard_map/ppermute | solution.py:17
  29.9 6.7 %tanh_convert_fusion.7 = (bf16[32,768]{1,0:T(8,128)(2,1)S(1)}, f32[32,768]{1,0:T(8,128)S(1)}) fusion(f32[32,768]{1,0:T(8,128)} %param.10, bf16[32,768]{1,0:T(8,128)(2,1)} %param.12, f32[32,768]{1,0:T(8,128)S(1)} %fusion.97, bf16[768,6144]{1,0:T(8,128)(2,1)} %param.14, bf16[32,3072]{1,0:T(8,128)(2,1)S(1)} %maximum_select_fusion.16, ...), kind=kOutput, calls=%fused_computation.144 | convolution fusion | flops 303955968 | bytes 10226689 | tf_op jit(solution)/shard_map/dot_general | solution.py:93
  39.4 3.4 %collective-permute-done.8 = bf16[32,1536]{1,0:T(8,128)(2,1)S(1)} collective-permute-done((bf16[32,1536]{1,0:T(8,128)(2,1)S(1)}, bf16[32,1536]{1,0:T(8,128)(2,1)S(1)}, u32[]{:S(2)}, u32[]{:S(2)}) %collective-permute-start.8) | collective-permute-done | bytes 98336 | tf_op jit(solution)/shard_map/ppermute | solution.py:17
  43.6 5.4 %collective-permute-done.9 = bf16[32,3072]{1,0:T(8,128)(2,1)S(1)} collective-permute-done((bf16[32,3072]{1,0:T(8,128)(2,1)S(1)}, bf16[32,3072]{1,0:T(8,128)(2,1)S(1)}, u32[]{:S(2)}, u32[]{:S(2)}) %collective-permute-start.9) | collective-permute-done | bytes 196640 | tf_op jit(solution)/shard_map/ppermute | solution.py:17
  49.0 2.9 %tanh_convert_fusion.6 = (bf16[32,768]{1,0:T(8,128)(2,1)S(1)}, f32[32,768]{1,0:T(8,128)S(1)}) fusion(f32[32,768]{1,0:T(8,128)S(1)} %get-tuple-element.3, bf16[32,768]{1,0:T(8,128)(2,1)S(1)} %copy-done.3, f32[32,768]{1,0:T(8,128)S(1)} %fusion.97, bf16[768,6144]{1,0:T(8,128)(2,1)S(1)} %copy-done.1, bf16[32,3072]{1,0:T(8,128)(2,1)S(1)} %maximum_select_fusion.17, ...), kind=kOutput, calls=%fused_computation.143 | convolution fusion | flops 303955968 | bytes 10226689 | tf_op jit(solution)/shard_map/dot_general | solution.py:93
  54.8 3.4 %collective-permute-done.11 = bf16[32,1536]{1,0:T(8,128)(2,1)S(1)} collective-permute-done((bf16[32,1536]{1,0:T(8,128)(2,1)S(1)}, bf16[32,1536]{1,0:T(8,128)(2,1)S(1)}, u32[]{:S(2)}, u32[]{:S(2)}) %collective-permute-start.11) | collective-permute-done | bytes 98336 | tf_op jit(solution)/shard_map/ppermute | solution.py:17
  59.0 5.4 %collective-permute-done.12 = bf16[32,3072]{1,0:T(8,128)(2,1)S(1)} collective-permute-done((bf16[32,3072]{1,0:T(8,128)(2,1)S(1)}, bf16[32,3072]{1,0:T(8,128)(2,1)S(1)}, u32[]{:S(2)}, u32[]{:S(2)}) %collective-permute-start.12) | collective-permute-done | bytes 196640 | tf_op jit(solution)/shard_map/ppermute | solution.py:17
  64.4 2.9 %tanh_convert_fusion.5 = (bf16[32,768]{1,0:T(8,128)(2,1)S(1)}, f32[32,768]{1,0:T(8,128)S(1)}) fusion(f32[32,768]{1,0:T(8,128)S(1)} %get-tuple-element.5, bf16[32,768]{1,0:T(8,128)(2,1)S(1)} %copy-done.3, f32[32,768]{1,0:T(8,128)S(1)} %fusion.97, bf16[768,6144]{1,0:T(8,128)(2,1)S(1)} %copy-done.1, bf16[32,3072]{1,0:T(8,128)(2,1)S(1)} %maximum_select_fusion.18, ...), kind=kOutput, calls=%fused_computation.142 | convolution fusion | flops 303955968 | bytes 10226689 | tf_op jit(solution)/shard_map/dot_general | solution.py:93
  70.2 3.4 %collective-permute-done.14 = bf16[32,1536]{1,0:T(8,128)(2,1)S(1)} collective-permute-done((bf16[32,1536]{1,0:T(8,128)(2,1)S(1)}, bf16[32,1536]{1,0:T(8,128)(2,1)S(1)}, u32[]{:S(2)}, u32[]{:S(2)}) %collective-permute-start.14) | collective-permute-done | bytes 98336 | tf_op jit(solution)/shard_map/ppermute | solution.py:17
  74.4 5.4 %collective-permute-done.15 = bf16[32,3072]{1,0:T(8,128)(2,1)S(1)} collective-permute-done((bf16[32,3072]{1,0:T(8,128)(2,1)S(1)}, bf16[32,3072]{1,0:T(8,128)(2,1)S(1)}, u32[]{:S(2)}, u32[]{:S(2)}) %collective-permute-start.15) | collective-permute-done | bytes 196640 | tf_op jit(solution)/shard_map/ppermute | solution.py:17
  79.9 2.9 %tanh_convert_fusion.4 = (bf16[32,768]{1,0:T(8,128)(2,1)S(1)}, f32[32,768]{1,0:T(8,128)S(1)}) fusion(f32[32,768]{1,0:T(8,128)S(1)} %get-tuple-element.7, bf16[32,768]{1,0:T(8,128)(2,1)S(1)} %copy-done.3, f32[32,768]{1,0:T(8,128)S(1)} %fusion.97, bf16[768,6144]{1,0:T(8,128)(2,1)S(1)} %copy-done.1, bf16[32,3072]{1,0:T(8,128)(2,1)S(1)} %maximum_select_fusion.19, ...), kind=kOutput, calls=%fused_computation.141 | convolution fusion | flops 303955968 | bytes 10226689 | tf_op jit(solution)/shard_map/dot_general | solution.py:93
  86.8 4.3 %collective-permute-done.19 = f32[1,32,768]{2,0,1:T(1,128)S(1)} collective-permute-done((f32[1,32,768]{2,0,1:T(1,128)S(1)}, f32[1,32,768]{2,0,1:T(1,128)S(1)}, u32[]{:S(2)}, u32[]{:S(2)}) %collective-permute-start.19) | collective-permute-done | bytes 98336 | tf_op jit(solution)/shard_map/ppermute | solution.py:17
  94.8 3.5 %collective-permute-done.21 = f32[32,768]{1,0:T(8,128)S(1)} collective-permute-done((f32[32,768]{1,0:T(8,128)S(1)}, f32[32,768]{1,0:T(8,128)S(1)}, u32[]{:S(2)}, u32[]{:S(2)}) %collective-permute-start.21) | collective-permute-done | bytes 98336 | tf_op jit(solution)/shard_map/ppermute | solution.py:17
  100.5 3.5 %collective-permute-done.22 = f32[32,768]{1,0:T(8,128)S(1)} collective-permute-done((f32[32,768]{1,0:T(8,128)S(1)}, f32[32,768]{1,0:T(8,128)S(1)}, u32[]{:S(2)}, u32[]{:S(2)}) %collective-permute-start.22) | collective-permute-done | bytes 98336 | tf_op jit(solution)/shard_map/ppermute | solution.py:17
  106.9 2.9 %tanh_convert_fusion.3 = (bf16[32,768]{1,0:T(8,128)(2,1)S(1)}, f32[32,768]{1,0:T(8,128)S(1)}) fusion(f32[32,768]{1,0:T(8,128)S(1)} %get-tuple-element.9, bf16[32,768]{1,0:T(8,128)(2,1)S(1)} %copy-done.3, f32[32,768]{1,0:T(8,128)S(1)} %fusion.98, bf16[768,6144]{1,0:T(8,128)(2,1)S(1)} %copy-done.1, bf16[32,3072]{1,0:T(8,128)(2,1)S(1)} %maximum_select_fusion.20, ...), kind=kOutput, calls=%fused_computation.139 | convolution fusion | flops 303955968 | bytes 10226689 | tf_op jit(solution)/shard_map/dot_general | solution.py:93
  112.6 3.4 %collective-permute-done.24 = bf16[32,1536]{1,0:T(8,128)(2,1)S(1)} collective-permute-done((bf16[32,1536]{1,0:T(8,128)(2,1)S(1)}, bf16[32,1536]{1,0:T(8,128)(2,1)S(1)}, u32[]{:S(2)}, u32[]{:S(2)}) %collective-permute-start.24) | collective-permute-done | bytes 98336 | tf_op jit(solution)/shard_map/ppermute | solution.py:17
  116.5 5.7 %collective-permute-done.25 = bf16[32,3072]{1,0:T(8,128)(2,1)S(1)} collective-permute-done((bf16[32,3072]{1,0:T(8,128)(2,1)S(1)}, bf16[32,3072]{1,0:T(8,128)(2,1)S(1)}, u32[]{:S(2)}, u32[]{:S(2)}) %collective-permute-start.25) | collective-permute-done | bytes 196640 | tf_op jit(solution)/shard_map/ppermute | solution.py:17
  128.0 3.4 %collective-permute-done.27 = bf16[32,1536]{1,0:T(8,128)(2,1)S(1)} collective-permute-done((bf16[32,1536]{1,0:T(8,128)(2,1)S(1)}, bf16[32,1536]{1,0:T(8,128)(2,1)S(1)}, u32[]{:S(2)}, u32[]{:S(2)}) %collective-permute-start.27) | collective-permute-done | bytes 98336 | tf_op jit(solution)/shard_map/ppermute | solution.py:17
  131.9 5.7 %collective-permute-done.28 = bf16[32,3072]{1,0:T(8,128)(2,1)S(1)} collective-permute-done((bf16[32,3072]{1,0:T(8,128)(2,1)S(1)}, bf16[32,3072]{1,0:T(8,128)(2,1)S(1)}, u32[]{:S(2)}, u32[]{:S(2)}) %collective-permute-start.28) | collective-permute-done | bytes 196640 | tf_op jit(solution)/shard_map/ppermute | solution.py:17
  143.4 3.4 %collective-permute-done.30 = bf16[32,1536]{1,0:T(8,128)(2,1)S(1)} collective-permute-done((bf16[32,1536]{1,0:T(8,128)(2,1)S(1)}, bf16[32,1536]{1,0:T(8,128)(2,1)S(1)}, u32[]{:S(2)}, u32[]{:S(2)}) %collective-permute-start.30) | collective-permute-done | bytes 98336 | tf_op jit(solution)/shard_map/ppermute | solution.py:17
  147.3 5.7 %collective-permute-done.31 = bf16[32,3072]{1,0:T(8,128)(2,1)S(1)} collective-permute-done((bf16[32,3072]{1,0:T(8,128)(2,1)S(1)}, bf16[32,3072]{1,0:T(8,128)(2,1)S(1)}, u32[]{:S(2)}, u32[]{:S(2)}) %collective-permute-start.31) | collective-permute-done | bytes 196640 | tf_op jit(solution)/shard_map/ppermute | solution.py:17
  (98 shorter events, 56.5 us)
Async XLA Ops:
  4.9 9.0 %collective-permute-start.3 = (f32[1,32,768]{2,0,1:T(1,128)S(1)}, f32[1,32,768]{2,0,1:T(1,128)S(1)}, u32[]{:S(2)}, u32[]{:S(2)}) collective-permute-start(f32[1,32,768]{2,0,1:T(1,128)S(1)} %broadcast_select_fusion.2), channel_id=1, source_target_pairs={{0,8},{8,0},{1,9},{9,1},{2,10},{10,2},{3,11},{11,3},{4,12},{12,4},... | collective-permute-start | bytes 294920 | tf_op jit(solution)/shard_map/ppermute | solution.py:17
  15.0 2.2 %collective-permute-start = (bf16[32,768]{1,0:T(8,128)(2,1)S(1)}, bf16[32,768]{1,0:T(8,128)(2,1)S(1)}, u32[]{:S(2)}, u32[]{:S(2)}) collective-permute-start(bf16[32,768]{1,0:T(8,128)(2,1)S(1)} %slice_bitcast_fusion), channel_id=1, source_target_pairs={{0,1},{1,0},{2,3},{3,2},{4,5},{5,4},{6,7},{7,6},{8,9},{9,8},{10,11... | collective-permute-start | bytes 147464 | tf_op jit(solution)/shard_map/ppermute | solution.py:17
  15.5 5.6 %collective-permute-start.5 = (f32[32,768]{1,0:T(8,128)S(1)}, f32[32,768]{1,0:T(8,128)S(1)}, u32[]{:S(2)}, u32[]{:S(2)}) collective-permute-start(f32[32,768]{1,0:T(8,128)S(1)} %fusion.120), channel_id=1, source_target_pairs={{0,2},{2,0},{1,3},{3,1},{4,6},{6,4},{5,7},{7,5},{8,10},{10,8},{9,1... | collective-permute-start | bytes 294920 | tf_op jit(solution)/shard_map/ppermute | solution.py:17
  17.2 5.3 %collective-permute-start.1 = (bf16[32,1536]{1,0:T(8,128)(2,1)S(1)}, bf16[32,1536]{1,0:T(8,128)(2,1)S(1)}, u32[]{:S(2)}, u32[]{:S(2)}) collective-permute-start(bf16[32,1536]{1,0:T(8,128)(2,1)S(1)} %maximum_select_fusion.24), channel_id=1, source_target_pairs={{0,2},{2,0},{1,3},{3,1},{4,6},{6,4},{5,7},{7,5},{8,10},{10,8},{9,1... | collective-permute-start | bytes 294920 | tf_op jit(solution)/shard_map/ppermute | solution.py:17
  21.2 5.7 %collective-permute-start.6 = (f32[32,768]{1,0:T(8,128)S(1)}, f32[32,768]{1,0:T(8,128)S(1)}, u32[]{:S(2)}, u32[]{:S(2)}) collective-permute-start(f32[32,768]{1,0:T(8,128)S(1)} %add.175), channel_id=1, source_target_pairs={{0,4},{4,0},{1,5},{5,1},{2,6},{6,2},{3,7},{7,3},{8,12},{12,8},{9,1... | collective-permute-start | bytes 294920 | tf_op jit(solution)/shard_map/ppermute | solution.py:17
  22.6 7.3 %collective-permute-start.2 = (bf16[32,3072]{1,0:T(8,128)(2,1)S(1)}, bf16[32,3072]{1,0:T(8,128)(2,1)S(1)}, u32[]{:S(2)}, u32[]{:S(2)}) collective-permute-start(bf16[32,3072]{1,0:T(8,128)(2,1)S(1)} %maximum_select_fusion.16), channel_id=1, source_target_pairs={{0,4},{4,0},{1,5},{5,1},{2,6},{6,2},{3,7},{7,3},{8,12},{12,8},{9,1... | collective-permute-start | bytes 589832 | tf_op jit(solution)/shard_map/ppermute | solution.py:17
  37.9 4.9 %collective-permute-start.8 = (bf16[32,1536]{1,0:T(8,128)(2,1)S(1)}, bf16[32,1536]{1,0:T(8,128)(2,1)S(1)}, u32[]{:S(2)}, u32[]{:S(2)}) collective-permute-start(bf16[32,1536]{1,0:T(8,128)(2,1)S(1)} %maximum_select_fusion.25), channel_id=1, source_target_pairs={{0,2},{2,0},{1,3},{3,1},{4,6},{6,4},{5,7},{7,5},{8,10},{10,8},{9,1... | collective-permute-start | bytes 294920 | tf_op jit(solution)/shard_map/ppermute | solution.py:17
  42.9 6.2 %collective-permute-start.9 = (bf16[32,3072]{1,0:T(8,128)(2,1)S(1)}, bf16[32,3072]{1,0:T(8,128)(2,1)S(1)}, u32[]{:S(2)}, u32[]{:S(2)}) collective-permute-start(bf16[32,3072]{1,0:T(8,128)(2,1)S(1)} %maximum_select_fusion.17), channel_id=1, source_target_pairs={{0,4},{4,0},{1,5},{5,1},{2,6},{6,2},{3,7},{7,3},{8,12},{12,8},{9,1... | collective-permute-start | bytes 589832 | tf_op jit(solution)/shard_map/ppermute | solution.py:17
  53.3 4.9 %collective-permute-start.11 = (bf16[32,1536]{1,0:T(8,128)(2,1)S(1)}, bf16[32,1536]{1,0:T(8,128)(2,1)S(1)}, u32[]{:S(2)}, u32[]{:S(2)}) collective-permute-start(bf16[32,1536]{1,0:T(8,128)(2,1)S(1)} %maximum_select_fusion.26), channel_id=1, source_target_pairs={{0,2},{2,0},{1,3},{3,1},{4,6},{6,4},{5,7},{7,5},{8,10},{10,8},{9,1... | collective-permute-start | bytes 294920 | tf_op jit(solution)/shard_map/ppermute | solution.py:17
  58.3 6.2 %collective-permute-start.12 = (bf16[32,3072]{1,0:T(8,128)(2,1)S(1)}, bf16[32,3072]{1,0:T(8,128)(2,1)S(1)}, u32[]{:S(2)}, u32[]{:S(2)}) collective-permute-start(bf16[32,3072]{1,0:T(8,128)(2,1)S(1)} %maximum_select_fusion.18), channel_id=1, source_target_pairs={{0,4},{4,0},{1,5},{5,1},{2,6},{6,2},{3,7},{7,3},{8,12},{12,8},{9,1... | collective-permute-start | bytes 589832 | tf_op jit(solution)/shard_map/ppermute | solution.py:17
  68.7 4.9 %collective-permute-start.14 = (bf16[32,1536]{1,0:T(8,128)(2,1)S(1)}, bf16[32,1536]{1,0:T(8,128)(2,1)S(1)}, u32[]{:S(2)}, u32[]{:S(2)}) collective-permute-start(bf16[32,1536]{1,0:T(8,128)(2,1)S(1)} %maximum_select_fusion.27), channel_id=1, source_target_pairs={{0,2},{2,0},{1,3},{3,1},{4,6},{6,4},{5,7},{7,5},{8,10},{10,8},{9,1... | collective-permute-start | bytes 294920 | tf_op jit(solution)/shard_map/ppermute | solution.py:17
  73.7 6.2 %collective-permute-start.15 = (bf16[32,3072]{1,0:T(8,128)(2,1)S(1)}, bf16[32,3072]{1,0:T(8,128)(2,1)S(1)}, u32[]{:S(2)}, u32[]{:S(2)}) collective-permute-start(bf16[32,3072]{1,0:T(8,128)(2,1)S(1)} %maximum_select_fusion.19), channel_id=1, source_target_pairs={{0,4},{4,0},{1,5},{5,1},{2,6},{6,2},{3,7},{7,3},{8,12},{12,8},{9,1... | collective-permute-start | bytes 589832 | tf_op jit(solution)/shard_map/ppermute | solution.py:17
  84.4 6.6 %collective-permute-start.19 = (f32[1,32,768]{2,0,1:T(1,128)S(1)}, f32[1,32,768]{2,0,1:T(1,128)S(1)}, u32[]{:S(2)}, u32[]{:S(2)}) collective-permute-start(f32[1,32,768]{2,0,1:T(1,128)S(1)} %broadcast_select_fusion), channel_id=1, source_target_pairs={{0,8},{8,0},{1,9},{9,1},{2,10},{10,2},{3,11},{11,3},{4,12},{12,4},... | collective-permute-start | bytes 294920 | tf_op jit(solution)/shard_map/ppermute | solution.py:17
  91.3 2.8 %collective-permute-start.16 = (bf16[32,768]{1,0:T(8,128)(2,1)S(1)}, bf16[32,768]{1,0:T(8,128)(2,1)S(1)}, u32[]{:S(2)}, u32[]{:S(2)}) collective-permute-start(bf16[32,768]{1,0:T(8,128)(2,1)S(1)} %get-tuple-element.8), channel_id=1, source_target_pairs={{0,1},{1,0},{2,3},{3,2},{4,5},{5,4},{6,7},{7,6},{8,9},{9,8},{10,11... | collective-permute-start | bytes 147464 | tf_op jit(solution)/shard_map/ppermute | solution.py:17
  92.6 5.7 %collective-permute-start.21 = (f32[32,768]{1,0:T(8,128)S(1)}, f32[32,768]{1,0:T(8,128)S(1)}, u32[]{:S(2)}, u32[]{:S(2)}) collective-permute-start(f32[32,768]{1,0:T(8,128)S(1)} %fusion.121), channel_id=1, source_target_pairs={{0,2},{2,0},{1,3},{3,1},{4,6},{6,4},{5,7},{7,5},{8,10},{10,8},{9,1... | collective-permute-start | bytes 294920 | tf_op jit(solution)/shard_map/ppermute | solution.py:17
  94.1 5.5 %collective-permute-start.17 = (bf16[32,1536]{1,0:T(8,128)(2,1)S(1)}, bf16[32,1536]{1,0:T(8,128)(2,1)S(1)}, u32[]{:S(2)}, u32[]{:S(2)}) collective-permute-start(bf16[32,1536]{1,0:T(8,128)(2,1)S(1)} %maximum_select_fusion.28), channel_id=1, source_target_pairs={{0,2},{2,0},{1,3},{3,1},{4,6},{6,4},{5,7},{7,5},{8,10},{10,8},{9,1... | collective-permute-start | bytes 294920 | tf_op jit(solution)/shard_map/ppermute | solution.py:17
  98.3 5.7 %collective-permute-start.22 = (f32[32,768]{1,0:T(8,128)S(1)}, f32[32,768]{1,0:T(8,128)S(1)}, u32[]{:S(2)}, u32[]{:S(2)}) collective-permute-start(f32[32,768]{1,0:T(8,128)S(1)} %add.195), channel_id=1, source_target_pairs={{0,4},{4,0},{1,5},{5,1},{2,6},{6,2},{3,7},{7,3},{8,12},{12,8},{9,1... | collective-permute-start | bytes 294920 | tf_op jit(solution)/shard_map/ppermute | solution.py:17
  99.7 7.2 %collective-permute-start.18 = (bf16[32,3072]{1,0:T(8,128)(2,1)S(1)}, bf16[32,3072]{1,0:T(8,128)(2,1)S(1)}, u32[]{:S(2)}, u32[]{:S(2)}) collective-permute-start(bf16[32,3072]{1,0:T(8,128)(2,1)S(1)} %maximum_select_fusion.20), channel_id=1, source_target_pairs={{0,4},{4,0},{1,5},{5,1},{2,6},{6,2},{3,7},{7,3},{8,12},{12,8},{9,1... | collective-permute-start | bytes 589832 | tf_op jit(solution)/shard_map/ppermute | solution.py:17
  111.1 4.9 %collective-permute-start.24 = (bf16[32,1536]{1,0:T(8,128)(2,1)S(1)}, bf16[32,1536]{1,0:T(8,128)(2,1)S(1)}, u32[]{:S(2)}, u32[]{:S(2)}) collective-permute-start(bf16[32,1536]{1,0:T(8,128)(2,1)S(1)} %maximum_select_fusion.29), channel_id=1, source_target_pairs={{0,2},{2,0},{1,3},{3,1},{4,6},{6,4},{5,7},{7,5},{8,10},{10,8},{9,1... | collective-permute-start | bytes 294920 | tf_op jit(solution)/shard_map/ppermute | solution.py:17
  116.1 6.2 %collective-permute-start.25 = (bf16[32,3072]{1,0:T(8,128)(2,1)S(1)}, bf16[32,3072]{1,0:T(8,128)(2,1)S(1)}, u32[]{:S(2)}, u32[]{:S(2)}) collective-permute-start(bf16[32,3072]{1,0:T(8,128)(2,1)S(1)} %maximum_select_fusion.21), channel_id=1, source_target_pairs={{0,4},{4,0},{1,5},{5,1},{2,6},{6,2},{3,7},{7,3},{8,12},{12,8},{9,1... | collective-permute-start | bytes 589832 | tf_op jit(solution)/shard_map/ppermute | solution.py:17
  126.5 4.9 %collective-permute-start.27 = (bf16[32,1536]{1,0:T(8,128)(2,1)S(1)}, bf16[32,1536]{1,0:T(8,128)(2,1)S(1)}, u32[]{:S(2)}, u32[]{:S(2)}) collective-permute-start(bf16[32,1536]{1,0:T(8,128)(2,1)S(1)} %maximum_select_fusion.30), channel_id=1, source_target_pairs={{0,2},{2,0},{1,3},{3,1},{4,6},{6,4},{5,7},{7,5},{8,10},{10,8},{9,1... | collective-permute-start | bytes 294920 | tf_op jit(solution)/shard_map/ppermute | solution.py:17
  131.5 6.2 %collective-permute-start.28 = (bf16[32,3072]{1,0:T(8,128)(2,1)S(1)}, bf16[32,3072]{1,0:T(8,128)(2,1)S(1)}, u32[]{:S(2)}, u32[]{:S(2)}) collective-permute-start(bf16[32,3072]{1,0:T(8,128)(2,1)S(1)} %maximum_select_fusion.22), channel_id=1, source_target_pairs={{0,4},{4,0},{1,5},{5,1},{2,6},{6,2},{3,7},{7,3},{8,12},{12,8},{9,1... | collective-permute-start | bytes 589832 | tf_op jit(solution)/shard_map/ppermute | solution.py:17
  141.9 4.9 %collective-permute-start.30 = (bf16[32,1536]{1,0:T(8,128)(2,1)S(1)}, bf16[32,1536]{1,0:T(8,128)(2,1)S(1)}, u32[]{:S(2)}, u32[]{:S(2)}) collective-permute-start(bf16[32,1536]{1,0:T(8,128)(2,1)S(1)} %maximum_select_fusion.31), channel_id=1, source_target_pairs={{0,2},{2,0},{1,3},{3,1},{4,6},{6,4},{5,7},{7,5},{8,10},{10,8},{9,1... | collective-permute-start | bytes 294920 | tf_op jit(solution)/shard_map/ppermute | solution.py:17
  146.9 6.2 %collective-permute-start.31 = (bf16[32,3072]{1,0:T(8,128)(2,1)S(1)}, bf16[32,3072]{1,0:T(8,128)(2,1)S(1)}, u32[]{:S(2)}, u32[]{:S(2)}) collective-permute-start(bf16[32,3072]{1,0:T(8,128)(2,1)S(1)} %maximum_select_fusion.23), channel_id=1, source_target_pairs={{0,4},{4,0},{1,5},{5,1},{2,6},{6,2},{3,7},{7,3},{8,12},{12,8},{9,1... | collective-permute-start | bytes 589832 | tf_op jit(solution)/shard_map/ppermute | solution.py:17
  (14 other events, 177.7 us)
where the time goes:
time: 157 us
  waiting for transfers between devices  89.8 us (57%)
  matrix products  33 us (21%)
  starting transfers between devices  28.4 us (18%)
  other arithmetic  2.62 us (2%)
  local copies, waits for them, and re-layouts  1.91 us (1%)
    ppermute x32, waiting for transfers between devices, from_partner(): return lax.ppermute(block, axis, route)  89.8 us
    ppermute x32, starting transfers between devices, from_partner(): return lax.ppermute(block, axis, route)  28.4 us
    dot_general x8, matrix products, body(): lax.dot_general(gathered_activity, w_recur, (((1,), (1,)), ((), ())), pre...  27.1 us
  transfers between devices with their start and end apart: 32, of which 29 were waited for; matrix products, arithmetic and copies ran while one was open for 2% of the time, Pallas kernels for 0%

commit v1 on v0

v1 whole, which is shorter than its diff:
```python
import jax
import jax.numpy as jnp
from jax import lax
from jax.sharding import PartitionSpec as P

INTERVALS = 2


def flipped(block, mask):
    count = lax.axis_size("area")
    return lax.ppermute(block, "area", [(i, i ^ mask) for i in range(count)])


def times_transposed(rates, weights):
    return lax.dot_general(
        rates, weights, (((1,), (1,)), ((), ())), preferred_element_type=jnp.float32
    )


def body(
    state_init,
    prior_interval_trace,
    drive_input,
    leak_rate,
    w_recur,
    w_send,
    w_recv,
    area_mask,
    coupling,
    delay_slot,
):
    ticks = prior_interval_trace.shape[0]
    trials, units = state_init.shape
    areas = area_mask.shape[1]
    split = lax.axis_size("area") // areas
    position = lax.axis_index("area")
    my_area = position // split
    direct = [2 * chip + 1 for chip in range(1, split // 2)]

    strength = area_mask.astype(jnp.float32) * coupling
    my_strength = lax.dynamic_index_in_dim(strength, my_area, 1, keepdims=False)
    my_slots = lax.dynamic_index_in_dim(delay_slot, my_area, 1, keepdims=False)
    drive = drive_input.astype(jnp.float32)
    leak = leak_rate[None, :]

    def column_block(mask):
        start = ((position ^ mask) % split) * units
        return lax.dynamic_slice_in_dim(w_recur, start, units, 1)

    def readouts(history):
        chosen = []
        for area in range(areas):
            pick = history[0]
            for tick in range(1, ticks):
                pick = jnp.where(my_slots[area] == tick, history[tick], pick)
            chosen.append(pick)
        read = jnp.dot(
            jnp.concatenate(chosen, 0), w_send, preferred_element_type=jnp.float32
        )
        return read.reshape(areas, trials, -1) * my_strength[:, None, None]

    def across_areas(contrib):
        level = areas // 2
        while level:
            half = contrib.shape[0] // 2
            upper = my_area // level % 2 == 1
            keep = jnp.where(upper, contrib[half:], contrib[:half])
            send = jnp.where(upper, contrib[:half], contrib[half:])
            contrib = keep + flipped(send.astype(jnp.bfloat16), split * level | 1)
            level //= 2
        return contrib[0]

    def received(contrib):
        contrib = across_areas(contrib)
        narrow = contrib.astype(jnp.bfloat16)
        for mask in direct:
            contrib = contrib + flipped(narrow, mask)
        contrib = contrib + flipped(contrib.astype(jnp.bfloat16), 1)
        return times_transposed(contrib.astype(jnp.bfloat16), w_recv)

    def recurrent(rates):
        total = times_transposed(rates, column_block(0))
        total = total + times_transposed(flipped(rates, 1), column_block(1))
        for mask in direct:
            there = flipped(rates, mask)
            total = total + times_transposed(there, column_block(mask))
            other = flipped(there, 1)
            total = total + times_transposed(other, column_block(mask ^ 1))
        return total

    potential = state_init
    history = [prior_interval_trace[tick] for tick in range(ticks)]
    rates = history[-1]
    for interval in range(INTERVALS):
        remote = received(readouts(history))
        fixed = remote + drive
        history = []
        for tick in range(ticks):
            potential = potential + leak * (-potential + recurrent(rates) + fixed)
            rates = jnp.tanh(potential).astype(jnp.bfloat16)
            history.append(rates)
    return potential, jnp.stack(history)


def solution(mesh):
    in_specs = (
        P("group", "area"),
        P(None, "group", "area"),
        P("group", "area"),
        P(("group", "area")),
        P(("group", "area"), None),
        P(("group", "area"), None),
        P(("group", "area"), None),
        P("group", None),
        P("group", None),
        P("group", None),
    )
    out_specs = (P("group", "area"), P(None, "group", "area"))
    return jax.shard_map(body, mesh=mesh, in_specs=in_specs, out_specs=out_specs, check_vma=False)
```

time: 157 us -> 111 us (0.71)
  waiting for transfers between devices: 89.8 us -> 9.42 us
  starting transfers between devices: 28.4 us -> 49 us
  matrix products: 33 us -> 42.1 us
  between operations: 1.01 us -> 4.98 us
    ppermute x32 -> x66, waiting for transfers between devices: 89.8 us -> 9.42 us  [flipped(): return lax.ppermute(block, 'area', [(i, i ^ mask) for i in range(count)])]
    ppermute x32 -> x66, starting transfers between devices: 28.4 us -> 49 us  [flipped(): return lax.ppermute(block, 'area', [(i, i ^ mask) for i in range(count)])]
    dot_general x14 -> x68, matrix products: 33 us -> 42.1 us  [the longest x66 41.5 us: times_transposed(): lax.dot_general(rates, weights, (((1,), (1,)), ((), ())), preferred_eleme...]
  transfers between devices with their start and end apart: 32 -> 66, of which waited for: 29 -> 20; matrix products, arithmetic and copies ran while one was open for 2% -> 37% of each run, Pallas kernels for 0% -> 0%
where the time goes in v1:
time: 111 us
  starting transfers between devices  49 us (44%)
  matrix products  42.1 us (38%)
  waiting for transfers between devices  9.42 us (8%)
  between operations  4.98 us (4%)
  local copies, waits for them, and re-layouts  2.79 us (3%)
  other arithmetic  2.62 us (2%)
    ppermute x66, starting transfers between devices, flipped(): return lax.ppermute(block, 'area', [(i, i ^ mask) for i in range(count)])  49 us
    dot_general x66, matrix products, times_transposed(): lax.dot_general(rates, weights, (((1,), (1,)), ((), ())), preferred_eleme...  41.5 us
    ppermute x66, waiting for transfers between devices, flipped(): return lax.ppermute(block, 'area', [(i, i ^ mask) for i in range(count)])  9.42 us
  transfers between devices with their start and end apart: 66, of which 20 were waited for; matrix products, arithmetic and copies ran while one was open for 37% of the time, Pallas kernels for 0%

profile of v1, /device:TPU:0, one launch (start us, length us, event | category | flops | bytes accessed | tf_op | source)
XLA Modules:
  0.0 111.0 jit_solution(1140613459251140735)
XLA Ops:
  2.0 2.6 %collective-permute-start.1 = (bf16[32,768]{1,0:T(8,128)(2,1)S(1)}, bf16[32,768]{1,0:T(8,128)(2,1)S(1)}, u32[]{:S(2)}, u32[]{:S(2)}) collective-permute-start(bf16[32,768]{1,0:T(8,128)(2,1)S(1)} %slice_bitcast_fusion), channel_id=1, source_target_pairs={{0,3},{1,2},{2,1},{3,0},{4,7},{5,6},{6,5},{7,4},{8,11},{9,10},{10,... | collective-permute-start | bytes 147464 | tf_op jit(solution)/shard_map/ppermute | solution.py:11
  13.3 2.8 %collective-permute-start.7 = (bf16[1,32,768]{2,1,0:T(8,128)(2,1)S(1)}, bf16[1,32,768]{2,1,0:T(8,128)(2,1)S(1)}, u32[]{:S(2)}, u32[]{:S(2)}) collective-permute-start(bf16[1,32,768]{2,1,0:T(8,128)(2,1)S(1)} %select_convert_fusion.1), channel_id=1, source_target_pairs={{0,9},{1,8},{2,11},{3,10},{4,13},{5,12},{6,15},{7,14},{8,1},{9,0},... | collective-permute-start | bytes 147464 | tf_op jit(solution)/shard_map/ppermute | solution.py:11
  16.0 1.7 %fusion.135 = f32[768,32]{0,1:T(8,128)S(1)} fusion(bf16[768,6144]{1,0:T(8,128)(2,1)} %param.14, s32[]{:T(128)S(6)} %select_n.344, bf16[4,32,768]{2,1,0:T(8,128)(2,1)} %param.11), kind=kOutput, calls=%fused_computation.177 | convolution fusion | flops 37748736 | bytes 1327108 | tf_op jit(solution)/shard_map/dot_general | solution.py:15
  18.0 3.2 %collective-permute-start.10 = (bf16[32,768]{1,0:T(8,128)(2,1)S(1)}, bf16[32,768]{1,0:T(8,128)(2,1)S(1)}, u32[]{:S(2)}, u32[]{:S(2)}) collective-permute-start(bf16[32,768]{1,0:T(8,128)(2,1)S(1)} %get-tuple-element.6), channel_id=1, source_target_pairs={{0,7},{1,6},{2,5},{3,4},{4,3},{5,2},{6,1},{7,0},{8,15},{9,14},{10,... | collective-permute-start | bytes 147464 | tf_op jit(solution)/shard_map/ppermute | solution.py:11
  21.8 1.9 %convolution_add_fusion.41 = f32[768,32]{0,1:T(8,128)S(1)} fusion(f32[768,32]{0,1:T(8,128)S(1)} %fusion.135, bf16[32,768]{1,0:T(8,128)(2,1)S(1)} %collective-permute-done, bf16[768,6144]{1,0:T(8,128)(2,1)} %param.14, s32[]{:T(128)S(6)} %select_n.346), kind=kOutput, calls=%fused_computation.90 | convolution fusion | flops 37773312 | bytes 1425412 | tf_op jit(solution)/shard_map/dot_general | solution.py:15
  23.9 2.2 %convolution_add_fusion.40 = f32[768,32]{0,1:T(8,128)S(1)} fusion(f32[768,32]{0,1:T(8,128)S(1)} %convolution_add_fusion.41, bf16[32,768]{1,0:T(8,128)(2,1)S(1)} %collective-permute-done.1, bf16[768,6144]{1,0:T(8,128)(2,1)} %param.14, s32[]{:T(128)S(6)} %select_n.348), kind=kOutput, calls=%fused_computation.89 | convolution fusion | flops 37773312 | bytes 1425412 | tf_op jit(solution)/shard_map/dot_general | solution.py:15
  26.3 1.7 %fusion.95 = f32[768,32]{0,1:T(8,128)S(1)} fusion(bf16[32,768]{1,0:T(8,128)(2,1)S(1)} %collective-permute-done.3, bf16[768,6144]{1,0:T(8,128)(2,1)} %param.14, s32[]{:T(128)S(6)} %select_n.352), kind=kOutput, calls=%fused_computation.137 | convolution fusion | flops 37748736 | bytes 1327108 | tf_op jit(solution)/shard_map/dot_general | solution.py:15
  28.4 1.7 %fusion.71 = f32[768,32]{0,1:T(8,128)S(1)} fusion(bf16[32,768]{1,0:T(8,128)(2,1)S(1)} %collective-permute-done.5, bf16[768,6144]{1,0:T(8,128)(2,1)} %param.14, s32[]{:T(128)S(6)} %select_n.356), kind=kOutput, calls=%fused_computation.113 | convolution fusion | flops 37748736 | bytes 1327108 | tf_op jit(solution)/shard_map/dot_general | solution.py:15
  30.8 1.7 %fusion.48 = f32[768,32]{0,1:T(8,128)S(1)} fusion(f32[768,32]{0,1:T(8,128)S(1)} %fusion.95, f32[768,32]{0,1:T(8,128)S(1)} %convolution_add_fusion.40, bf16[32,768]{1,0:T(8,128)(2,1)S(1)} %collective-permute-done.2, bf16[768,6144]{1,0:T(8,128)(2,1)} %param.14, s32[]{:T(128)S(6)} %select_n.350), kind=kOutput, calls=%fused_computation.88 | convolution fusion | flops 37797888 | bytes 1523716 | tf_op jit(solution)/shard_map/dot_general | solution.py:15
  32.6 1.8 %fusion.47 = f32[768,32]{0,1:T(8,128)S(1)} fusion(f32[768,32]{0,1:T(8,128)S(1)} %fusion.71, f32[768,32]{0,1:T(8,128)S(1)} %fusion.48, bf16[32,768]{1,0:T(8,128)(2,1)S(1)} %collective-permute-done.4, bf16[768,6144]{1,0:T(8,128)(2,1)} %param.14, s32[]{:T(128)S(6)} %select_n.354), kind=kOutput, calls=%fused_computation.86 | convolution fusion | flops 37797888 | bytes 1523716 | tf_op jit(solution)/shard_map/dot_general | solution.py:15
  35.8 2.1 %collective-permute-start.17 = (bf16[32,768]{1,0:T(8,128)(2,1)S(1)}, bf16[32,768]{1,0:T(8,128)(2,1)S(1)}, u32[]{:S(2)}, u32[]{:S(2)}) collective-permute-start(bf16[32,768]{1,0:T(8,128)(2,1)S(1)} %get-tuple-element.12), channel_id=1, source_target_pairs={{0,7},{1,6},{2,5},{3,4},{4,3},{5,2},{6,1},{7,0},{8,15},{9,14},{10,... | collective-permute-start | bytes 147464 | tf_op jit(solution)/shard_map/ppermute | solution.py:11
  46.0 1.3 %collective-permute-start.24 = (bf16[32,768]{1,0:T(8,128)(2,1)S(1)}, bf16[32,768]{1,0:T(8,128)(2,1)S(1)}, u32[]{:S(2)}, u32[]{:S(2)}) collective-permute-start(bf16[32,768]{1,0:T(8,128)(2,1)S(1)} %get-tuple-element.14), channel_id=1, source_target_pairs={{0,7},{1,6},{2,5},{3,4},{4,3},{5,2},{6,1},{7,0},{8,15},{9,14},{10,... | collective-permute-start | bytes 147464 | tf_op jit(solution)/shard_map/ppermute | solution.py:11
  48.5 1.3 %collective-permute-start.22 = (bf16[32,768]{1,0:T(8,128)(2,1)S(1)}, bf16[32,768]{1,0:T(8,128)(2,1)S(1)}, u32[]{:S(2)}, u32[]{:S(2)}) collective-permute-start(bf16[32,768]{1,0:T(8,128)(2,1)S(1)} %get-tuple-element.14), channel_id=1, source_target_pairs={{0,5},{1,4},{2,7},{3,6},{4,1},{5,0},{6,3},{7,2},{8,13},{9,12},{10,... | collective-permute-start | bytes 147464 | tf_op jit(solution)/shard_map/ppermute | solution.py:11
  55.5 1.5 %collective-permute-start.31 = (bf16[32,768]{1,0:T(8,128)(2,1)S(1)}, bf16[32,768]{1,0:T(8,128)(2,1)S(1)}, u32[]{:S(2)}, u32[]{:S(2)}) collective-permute-start(bf16[32,768]{1,0:T(8,128)(2,1)S(1)} %get-tuple-element.16), channel_id=1, source_target_pairs={{0,7},{1,6},{2,5},{3,4},{4,3},{5,2},{6,1},{7,0},{8,15},{9,14},{10,... | collective-permute-start | bytes 147464 | tf_op jit(solution)/shard_map/ppermute | solution.py:11
  57.9 1.4 %collective-permute-start.29 = (bf16[32,768]{1,0:T(8,128)(2,1)S(1)}, bf16[32,768]{1,0:T(8,128)(2,1)S(1)}, u32[]{:S(2)}, u32[]{:S(2)}) collective-permute-start(bf16[32,768]{1,0:T(8,128)(2,1)S(1)} %get-tuple-element.16), channel_id=1, source_target_pairs={{0,5},{1,4},{2,7},{3,6},{4,1},{5,0},{6,3},{7,2},{8,13},{9,12},{10,... | collective-permute-start | bytes 147464 | tf_op jit(solution)/shard_map/ppermute | solution.py:11
  65.4 3.3 %collective-permute-start.40 = (bf16[1,32,768]{2,1,0:T(8,128)(2,1)S(1)}, bf16[1,32,768]{2,1,0:T(8,128)(2,1)S(1)}, u32[]{:S(2)}, u32[]{:S(2)}) collective-permute-start(bf16[1,32,768]{2,1,0:T(8,128)(2,1)S(1)} %select_convert_fusion), channel_id=1, source_target_pairs={{0,9},{1,8},{2,11},{3,10},{4,13},{5,12},{6,15},{7,14},{8,1},{9,0},... | collective-permute-start | bytes 147464 | tf_op jit(solution)/shard_map/ppermute | solution.py:11
  71.1 1.4 %collective-permute-start.38 = (bf16[32,768]{1,0:T(8,128)(2,1)S(1)}, bf16[32,768]{1,0:T(8,128)(2,1)S(1)}, u32[]{:S(2)}, u32[]{:S(2)}) collective-permute-start(bf16[32,768]{1,0:T(8,128)(2,1)S(1)} %get-tuple-element.5), channel_id=1, source_target_pairs={{0,7},{1,6},{2,5},{3,4},{4,3},{5,2},{6,1},{7,0},{8,15},{9,14},{10,... | collective-permute-start | bytes 147464 | tf_op jit(solution)/shard_map/ppermute | solution.py:11
  73.0 1.3 %collective-permute-start.42 = (bf16[32,768]{1,0:T(8,128)(2,1)S(1)}, bf16[32,768]{1,0:T(8,128)(2,1)S(1)}, u32[]{:S(2)}, u32[]{:S(2)}) collective-permute-start(bf16[32,768]{1,0:T(8,128)(2,1)S(1)} %get-tuple-element.2), channel_id=1, source_target_pairs={{0,5},{1,4},{2,7},{3,6},{4,1},{5,0},{6,3},{7,2},{8,13},{9,12},{10,... | collective-permute-start | bytes 147464 | tf_op jit(solution)/shard_map/ppermute | solution.py:11
  74.8 1.4 %collective-permute-start.43 = (bf16[32,768]{1,0:T(8,128)(2,1)S(1)}, bf16[32,768]{1,0:T(8,128)(2,1)S(1)}, u32[]{:S(2)}, u32[]{:S(2)}) collective-permute-start(bf16[32,768]{1,0:T(8,128)(2,1)S(1)} %get-tuple-element.2), channel_id=1, source_target_pairs={{0,7},{1,6},{2,5},{3,4},{4,3},{5,2},{6,1},{7,0},{8,15},{9,14},{10,... | collective-permute-start | bytes 147464 | tf_op jit(solution)/shard_map/ppermute | solution.py:11
  81.7 1.5 %collective-permute-start.50 = (bf16[32,768]{1,0:T(8,128)(2,1)S(1)}, bf16[32,768]{1,0:T(8,128)(2,1)S(1)}, u32[]{:S(2)}, u32[]{:S(2)}) collective-permute-start(bf16[32,768]{1,0:T(8,128)(2,1)S(1)} %get-tuple-element.19), channel_id=1, source_target_pairs={{0,7},{1,6},{2,5},{3,4},{4,3},{5,2},{6,1},{7,0},{8,15},{9,14},{10,... | collective-permute-start | bytes 147464 | tf_op jit(solution)/shard_map/ppermute | solution.py:11
  91.3 1.3 %collective-permute-start.57 = (bf16[32,768]{1,0:T(8,128)(2,1)S(1)}, bf16[32,768]{1,0:T(8,128)(2,1)S(1)}, u32[]{:S(2)}, u32[]{:S(2)}) collective-permute-start(bf16[32,768]{1,0:T(8,128)(2,1)S(1)} %get-tuple-element.21), channel_id=1, source_target_pairs={{0,7},{1,6},{2,5},{3,4},{4,3},{5,2},{6,1},{7,0},{8,15},{9,14},{10,... | collective-permute-start | bytes 147464 | tf_op jit(solution)/shard_map/ppermute | solution.py:11
  93.6 1.6 %collective-permute-start.55 = (bf16[32,768]{1,0:T(8,128)(2,1)S(1)}, bf16[32,768]{1,0:T(8,128)(2,1)S(1)}, u32[]{:S(2)}, u32[]{:S(2)}) collective-permute-start(bf16[32,768]{1,0:T(8,128)(2,1)S(1)} %get-tuple-element.21), channel_id=1, source_target_pairs={{0,5},{1,4},{2,7},{3,6},{4,1},{5,0},{6,3},{7,2},{8,13},{9,12},{10,... | collective-permute-start | bytes 147464 | tf_op jit(solution)/shard_map/ppermute | solution.py:11
  100.6 1.5 %collective-permute-start.64 = (bf16[32,768]{1,0:T(8,128)(2,1)S(1)}, bf16[32,768]{1,0:T(8,128)(2,1)S(1)}, u32[]{:S(2)}, u32[]{:S(2)}) collective-permute-start(bf16[32,768]{1,0:T(8,128)(2,1)S(1)} %get-tuple-element.23), channel_id=1, source_target_pairs={{0,7},{1,6},{2,5},{3,4},{4,3},{5,2},{6,1},{7,0},{8,15},{9,14},{10,... | collective-permute-start | bytes 147464 | tf_op jit(solution)/shard_map/ppermute | solution.py:11
  103.2 1.3 %collective-permute-start.62 = (bf16[32,768]{1,0:T(8,128)(2,1)S(1)}, bf16[32,768]{1,0:T(8,128)(2,1)S(1)}, u32[]{:S(2)}, u32[]{:S(2)}) collective-permute-start(bf16[32,768]{1,0:T(8,128)(2,1)S(1)} %get-tuple-element.23), channel_id=1, source_target_pairs={{0,5},{1,4},{2,7},{3,6},{4,1},{5,0},{6,3},{7,2},{8,13},{9,12},{10,... | collective-permute-start | bytes 147464 | tf_op jit(solution)/shard_map/ppermute | solution.py:11
  (207 shorter events, 62.3 us)
Async XLA Ops:
  1.5 19.7 %collective-permute-start = (bf16[32,768]{1,0:T(8,128)(2,1)S(1)}, bf16[32,768]{1,0:T(8,128)(2,1)S(1)}, u32[]{:S(2)}, u32[]{:S(2)}) collective-permute-start(bf16[32,768]{1,0:T(8,128)(2,1)S(1)} %slice_bitcast_fusion), channel_id=1, source_target_pairs={{0,1},{1,0},{2,3},{3,2},{4,5},{5,4},{6,7},{7,6},{8,9},{9,8},{10,11... | collective-permute-start | bytes 147464 | tf_op jit(solution)/shard_map/ppermute | solution.py:11
  2.0 21.6 %collective-permute-start.1 = (bf16[32,768]{1,0:T(8,128)(2,1)S(1)}, bf16[32,768]{1,0:T(8,128)(2,1)S(1)}, u32[]{:S(2)}, u32[]{:S(2)}) collective-permute-start(bf16[32,768]{1,0:T(8,128)(2,1)S(1)} %slice_bitcast_fusion), channel_id=1, source_target_pairs={{0,3},{1,2},{2,1},{3,0},{4,7},{5,6},{6,5},{7,4},{8,11},{9,10},{10,... | collective-permute-start | bytes 147464 | tf_op jit(solution)/shard_map/ppermute | solution.py:11
  4.7 21.5 %collective-permute-start.3 = (bf16[32,768]{1,0:T(8,128)(2,1)S(1)}, bf16[32,768]{1,0:T(8,128)(2,1)S(1)}, u32[]{:S(2)}, u32[]{:S(2)}) collective-permute-start(bf16[32,768]{1,0:T(8,128)(2,1)S(1)} %slice_bitcast_fusion), channel_id=1, source_target_pairs={{0,5},{1,4},{2,7},{3,6},{4,1},{5,0},{6,3},{7,2},{8,13},{9,12},{10,... | collective-permute-start | bytes 147464 | tf_op jit(solution)/shard_map/ppermute | solution.py:11
  5.8 22.2 %collective-permute-start.5 = (bf16[32,768]{1,0:T(8,128)(2,1)S(1)}, bf16[32,768]{1,0:T(8,128)(2,1)S(1)}, u32[]{:S(2)}, u32[]{:S(2)}) collective-permute-start(bf16[32,768]{1,0:T(8,128)(2,1)S(1)} %slice_bitcast_fusion), channel_id=1, source_target_pairs={{0,7},{1,6},{2,5},{3,4},{4,3},{5,2},{6,1},{7,0},{8,15},{9,14},{10,... | collective-permute-start | bytes 147464 | tf_op jit(solution)/shard_map/ppermute | solution.py:11
  13.3 4.7 %collective-permute-start.7 = (bf16[1,32,768]{2,1,0:T(8,128)(2,1)S(1)}, bf16[1,32,768]{2,1,0:T(8,128)(2,1)S(1)}, u32[]{:S(2)}, u32[]{:S(2)}) collective-permute-start(bf16[1,32,768]{2,1,0:T(8,128)(2,1)S(1)} %select_convert_fusion.1), channel_id=1, source_target_pairs={{0,9},{1,8},{2,11},{3,10},{4,13},{5,12},{6,15},{7,14},{8,1},{9,0},... | collective-permute-start | bytes 147464 | tf_op jit(solution)/shard_map/ppermute | solution.py:11
  18.0 12.2 %collective-permute-start.10 = (bf16[32,768]{1,0:T(8,128)(2,1)S(1)}, bf16[32,768]{1,0:T(8,128)(2,1)S(1)}, u32[]{:S(2)}, u32[]{:S(2)}) collective-permute-start(bf16[32,768]{1,0:T(8,128)(2,1)S(1)} %get-tuple-element.6), channel_id=1, source_target_pairs={{0,7},{1,6},{2,5},{3,4},{4,3},{5,2},{6,1},{7,0},{8,15},{9,14},{10,... | collective-permute-start | bytes 147464 | tf_op jit(solution)/shard_map/ppermute | solution.py:11
  21.2 9.0 %collective-permute-start.8 = (bf16[32,768]{1,0:T(8,128)(2,1)S(1)}, bf16[32,768]{1,0:T(8,128)(2,1)S(1)}, u32[]{:S(2)}, u32[]{:S(2)}) collective-permute-start(bf16[32,768]{1,0:T(8,128)(2,1)S(1)} %get-tuple-element.6), channel_id=1, source_target_pairs={{0,3},{1,2},{2,1},{3,0},{4,7},{5,6},{6,5},{7,4},{8,11},{9,10},{10,... | collective-permute-start | bytes 147464 | tf_op jit(solution)/shard_map/ppermute | solution.py:11
  23.7 6.6 %collective-permute-start.9 = (bf16[32,768]{1,0:T(8,128)(2,1)S(1)}, bf16[32,768]{1,0:T(8,128)(2,1)S(1)}, u32[]{:S(2)}, u32[]{:S(2)}) collective-permute-start(bf16[32,768]{1,0:T(8,128)(2,1)S(1)} %get-tuple-element.6), channel_id=1, source_target_pairs={{0,5},{1,4},{2,7},{3,6},{4,1},{5,0},{6,3},{7,2},{8,13},{9,12},{10,... | collective-permute-start | bytes 147464 | tf_op jit(solution)/shard_map/ppermute | solution.py:11
  26.1 4.7 %collective-permute-start.2 = (bf16[32,768]{1,0:T(8,128)(2,1)S(1)}, bf16[32,768]{1,0:T(8,128)(2,1)S(1)}, u32[]{:S(2)}, u32[]{:S(2)}) collective-permute-start(bf16[32,768]{1,0:T(8,128)(2,1)S(1)} %collective-permute-done.1), channel_id=1, source_target_pairs={{0,1},{1,0},{2,3},{3,2},{4,5},{5,4},{6,7},{7,6},{8,9},{9,8},{10,11... | collective-permute-start | bytes 147464 | tf_op jit(solution)/shard_map/ppermute | solution.py:11
  30.2 4.7 %collective-permute-start.6 = (bf16[32,768]{1,0:T(8,128)(2,1)S(1)}, bf16[32,768]{1,0:T(8,128)(2,1)S(1)}, u32[]{:S(2)}, u32[]{:S(2)}) collective-permute-start(bf16[32,768]{1,0:T(8,128)(2,1)S(1)} %collective-permute-done.5), channel_id=1, source_target_pairs={{0,1},{1,0},{2,3},{3,2},{4,5},{5,4},{6,7},{7,6},{8,9},{9,8},{10,11... | collective-permute-start | bytes 147464 | tf_op jit(solution)/shard_map/ppermute | solution.py:11
  35.8 4.7 %collective-permute-start.17 = (bf16[32,768]{1,0:T(8,128)(2,1)S(1)}, bf16[32,768]{1,0:T(8,128)(2,1)S(1)}, u32[]{:S(2)}, u32[]{:S(2)}) collective-permute-start(bf16[32,768]{1,0:T(8,128)(2,1)S(1)} %get-tuple-element.12), channel_id=1, source_target_pairs={{0,7},{1,6},{2,5},{3,4},{4,3},{5,2},{6,1},{7,0},{8,15},{9,14},{10,... | collective-permute-start | bytes 147464 | tf_op jit(solution)/shard_map/ppermute | solution.py:11
  39.0 4.7 %collective-permute-start.15 = (bf16[32,768]{1,0:T(8,128)(2,1)S(1)}, bf16[32,768]{1,0:T(8,128)(2,1)S(1)}, u32[]{:S(2)}, u32[]{:S(2)}) collective-permute-start(bf16[32,768]{1,0:T(8,128)(2,1)S(1)} %get-tuple-element.12), channel_id=1, source_target_pairs={{0,5},{1,4},{2,7},{3,6},{4,1},{5,0},{6,3},{7,2},{8,13},{9,12},{10,... | collective-permute-start | bytes 147464 | tf_op jit(solution)/shard_map/ppermute | solution.py:11
  48.5 4.6 %collective-permute-start.22 = (bf16[32,768]{1,0:T(8,128)(2,1)S(1)}, bf16[32,768]{1,0:T(8,128)(2,1)S(1)}, u32[]{:S(2)}, u32[]{:S(2)}) collective-permute-start(bf16[32,768]{1,0:T(8,128)(2,1)S(1)} %get-tuple-element.14), channel_id=1, source_target_pairs={{0,5},{1,4},{2,7},{3,6},{4,1},{5,0},{6,3},{7,2},{8,13},{9,12},{10,... | collective-permute-start | bytes 147464 | tf_op jit(solution)/shard_map/ppermute | solution.py:11
  57.9 4.7 %collective-permute-start.29 = (bf16[32,768]{1,0:T(8,128)(2,1)S(1)}, bf16[32,768]{1,0:T(8,128)(2,1)S(1)}, u32[]{:S(2)}, u32[]{:S(2)}) collective-permute-start(bf16[32,768]{1,0:T(8,128)(2,1)S(1)} %get-tuple-element.16), channel_id=1, source_target_pairs={{0,5},{1,4},{2,7},{3,6},{4,1},{5,0},{6,3},{7,2},{8,13},{9,12},{10,... | collective-permute-start | bytes 147464 | tf_op jit(solution)/shard_map/ppermute | solution.py:11
  65.4 7.1 %collective-permute-start.40 = (bf16[1,32,768]{2,1,0:T(8,128)(2,1)S(1)}, bf16[1,32,768]{2,1,0:T(8,128)(2,1)S(1)}, u32[]{:S(2)}, u32[]{:S(2)}) collective-permute-start(bf16[1,32,768]{2,1,0:T(8,128)(2,1)S(1)} %select_convert_fusion), channel_id=1, source_target_pairs={{0,9},{1,8},{2,11},{3,10},{4,13},{5,12},{6,15},{7,14},{8,1},{9,0},... | collective-permute-start | bytes 147464 | tf_op jit(solution)/shard_map/ppermute | solution.py:11
  69.4 5.3 %collective-permute-start.34 = (bf16[32,768]{1,0:T(8,128)(2,1)S(1)}, bf16[32,768]{1,0:T(8,128)(2,1)S(1)}, u32[]{:S(2)}, u32[]{:S(2)}) collective-permute-start(bf16[32,768]{1,0:T(8,128)(2,1)S(1)} %get-tuple-element.5), channel_id=1, source_target_pairs={{0,3},{1,2},{2,1},{3,0},{4,7},{5,6},{6,5},{7,4},{8,11},{9,10},{10,... | collective-permute-start | bytes 147464 | tf_op jit(solution)/shard_map/ppermute | solution.py:11
  69.9 6.8 %collective-permute-start.36 = (bf16[32,768]{1,0:T(8,128)(2,1)S(1)}, bf16[32,768]{1,0:T(8,128)(2,1)S(1)}, u32[]{:S(2)}, u32[]{:S(2)}) collective-permute-start(bf16[32,768]{1,0:T(8,128)(2,1)S(1)} %get-tuple-element.5), channel_id=1, source_target_pairs={{0,5},{1,4},{2,7},{3,6},{4,1},{5,0},{6,3},{7,2},{8,13},{9,12},{10,... | collective-permute-start | bytes 147464 | tf_op jit(solution)/shard_map/ppermute | solution.py:11
  71.1 6.4 %collective-permute-start.38 = (bf16[32,768]{1,0:T(8,128)(2,1)S(1)}, bf16[32,768]{1,0:T(8,128)(2,1)S(1)}, u32[]{:S(2)}, u32[]{:S(2)}) collective-permute-start(bf16[32,768]{1,0:T(8,128)(2,1)S(1)} %get-tuple-element.5), channel_id=1, source_target_pairs={{0,7},{1,6},{2,5},{3,4},{4,3},{5,2},{6,1},{7,0},{8,15},{9,14},{10,... | collective-permute-start | bytes 147464 | tf_op jit(solution)/shard_map/ppermute | solution.py:11
  72.5 5.6 %collective-permute-start.41 = (bf16[32,768]{1,0:T(8,128)(2,1)S(1)}, bf16[32,768]{1,0:T(8,128)(2,1)S(1)}, u32[]{:S(2)}, u32[]{:S(2)}) collective-permute-start(bf16[32,768]{1,0:T(8,128)(2,1)S(1)} %get-tuple-element.2), channel_id=1, source_target_pairs={{0,3},{1,2},{2,1},{3,0},{4,7},{5,6},{6,5},{7,4},{8,11},{9,10},{10,... | collective-permute-start | bytes 147464 | tf_op jit(solution)/shard_map/ppermute | solution.py:11
  73.0 5.5 %collective-permute-start.42 = (bf16[32,768]{1,0:T(8,128)(2,1)S(1)}, bf16[32,768]{1,0:T(8,128)(2,1)S(1)}, u32[]{:S(2)}, u32[]{:S(2)}) collective-permute-start(bf16[32,768]{1,0:T(8,128)(2,1)S(1)} %get-tuple-element.2), channel_id=1, source_target_pairs={{0,5},{1,4},{2,7},{3,6},{4,1},{5,0},{6,3},{7,2},{8,13},{9,12},{10,... | collective-permute-start | bytes 147464 | tf_op jit(solution)/shard_map/ppermute | solution.py:11
  74.8 4.6 %collective-permute-start.43 = (bf16[32,768]{1,0:T(8,128)(2,1)S(1)}, bf16[32,768]{1,0:T(8,128)(2,1)S(1)}, u32[]{:S(2)}, u32[]{:S(2)}) collective-permute-start(bf16[32,768]{1,0:T(8,128)(2,1)S(1)} %get-tuple-element.2), channel_id=1, source_target_pairs={{0,7},{1,6},{2,5},{3,4},{4,3},{5,2},{6,1},{7,0},{8,15},{9,14},{10,... | collective-permute-start | bytes 147464 | tf_op jit(solution)/shard_map/ppermute | solution.py:11
  84.3 4.7 %collective-permute-start.48 = (bf16[32,768]{1,0:T(8,128)(2,1)S(1)}, bf16[32,768]{1,0:T(8,128)(2,1)S(1)}, u32[]{:S(2)}, u32[]{:S(2)}) collective-permute-start(bf16[32,768]{1,0:T(8,128)(2,1)S(1)} %get-tuple-element.19), channel_id=1, source_target_pairs={{0,5},{1,4},{2,7},{3,6},{4,1},{5,0},{6,3},{7,2},{8,13},{9,12},{10,... | collective-permute-start | bytes 147464 | tf_op jit(solution)/shard_map/ppermute | solution.py:11
  93.6 4.7 %collective-permute-start.55 = (bf16[32,768]{1,0:T(8,128)(2,1)S(1)}, bf16[32,768]{1,0:T(8,128)(2,1)S(1)}, u32[]{:S(2)}, u32[]{:S(2)}) collective-permute-start(bf16[32,768]{1,0:T(8,128)(2,1)S(1)} %get-tuple-element.21), channel_id=1, source_target_pairs={{0,5},{1,4},{2,7},{3,6},{4,1},{5,0},{6,3},{7,2},{8,13},{9,12},{10,... | collective-permute-start | bytes 147464 | tf_op jit(solution)/shard_map/ppermute | solution.py:11
  103.2 4.7 %collective-permute-start.62 = (bf16[32,768]{1,0:T(8,128)(2,1)S(1)}, bf16[32,768]{1,0:T(8,128)(2,1)S(1)}, u32[]{:S(2)}, u32[]{:S(2)}) collective-permute-start(bf16[32,768]{1,0:T(8,128)(2,1)S(1)} %get-tuple-element.23), channel_id=1, source_target_pairs={{0,5},{1,4},{2,7},{3,6},{4,1},{5,0},{6,3},{7,2},{8,13},{9,12},{10,... | collective-permute-start | bytes 147464 | tf_op jit(solution)/shard_map/ppermute | solution.py:11
  (49 other events, 197.4 us)
